TPU v7x, 512 devices: a whole 4x8x8 slice. The times are simulated.
512 devices in a mesh: seq: 32 (over y, z_hi, core), head: 16 (over x, z_lo).
Axes of the slice: x: 4, y: 8, z: 8 (z_hi: 2, z_lo: 4; z = z_hi * 4 + z_lo), core: 2. Of those that a mesh axis runs over, the one named last changes fastest.
Arguments:
- query_new: bfloat16 [4096, 6144], P('seq', 'head'), may hold values from -18 to 18
- key_new: bfloat16 [4096, 6144], P('seq', 'head'), may hold values from -4 to 4
- value_new: bfloat16 [4096, 6144], P('seq', 'head'), may hold values from -6 to 6
- cache_keys: bfloat16 [2048, 6144], P(('seq', 'head')), may hold values from -448 to 448
- cache_values: bfloat16 [2048, 6144], P(('seq', 'head')), may hold values from -448 to 448
- key_exponent: int32 [512, 48], P(('seq', 'head')), may hold values from -9 to -6
- value_exponent: int32 [512, 48], P(('seq', 'head')), may hold values from -9 to -6
- block_mask: int32 [64, 64], replicated, may hold values 0 or 1
Outputs:
- attended: bfloat16 [4096, 6144], P('seq', 'head')
All inputs are finite; a program needn't handle non-finite values.
Results may differ from a plain program's by a relative error of at most 0.0065.
Values may be sent and summed in bfloat16 or wider, within the bound.
A program may use at most 64 MiB of HBM per device.

v0:
```python
import math

import jax
import jax.numpy as jnp
from jax import lax
from jax.sharding import Mesh
from jax.sharding import PartitionSpec as P

DH = 128
QBLK = 64
CBLK = 32
SBLK = 4
SEQ = ("seq_0", "seq_1", "seq_2")
SEQ_HEAD = ("seq_0", "seq_1", "seq_2", "head")


def joined_along(tiles, dim):
    shape = list(tiles.shape[1:])
    shape[dim] *= tiles.shape[0]
    return jnp.moveaxis(tiles, 0, dim).reshape(shape)


def gather_in_order(array, axes, turns):
    tiles = array
    for k in turns:
        tiles = lax.all_gather(tiles, axes[k])
    done = turns[::-1]
    back = [done.index(k) for k in range(len(axes))]
    tiles = tiles.transpose(*back, *range(len(axes), tiles.ndim))
    return tiles.reshape(-1, *array.shape)


def gathered_by_axis(array, axes, turns, dim):
    return joined_along(gather_in_order(array, axes, turns), dim)


def dequantize(mantissa, exponent):
    head_count = mantissa.shape[1] // DH
    block_rows = mantissa.shape[0] // SBLK
    factor = jnp.exp2(exponent.astype(jnp.float32))
    scaled = (
        mantissa.astype(jnp.float32).reshape(block_rows, SBLK, head_count, DH)
        * factor[:, None, :, None]
    )
    return scaled.reshape(mantissa.shape).astype(jnp.bfloat16)


def per_device(
    query_new,
    key_new,
    value_new,
    cache_keys,
    cache_values,
    key_exponent,
    value_exponent,
    block_mask,
):
    tok_rows = query_new.shape[0]
    width_dev = query_new.shape[1]
    heads_dev = width_dev // DH
    inv_root = 1.0 / math.sqrt(DH)
    key_cache, value_cache = (
        lax.all_to_all(
            dequantize(cache_keys, key_exponent), "head", split_axis=1, concat_axis=0, tiled=True
        ),
        lax.all_to_all(
            dequantize(cache_values, value_exponent),
            "head",
            split_axis=1,
            concat_axis=0,
            tiled=True,
        ),
    )
    cache_rows = key_cache.shape[0]
    seq_index = lax.axis_index(SEQ)
    mask_blocks = block_mask.shape[1]
    block_ids = jnp.arange(mask_blocks, dtype=jnp.int32)
    local_keys = jnp.concatenate([key_cache, key_new], axis=0)
    local_values = jnp.concatenate([value_cache, value_new], axis=0)
    shard_rows = cache_rows + tok_rows
    queries = query_new.reshape(tok_rows, heads_dev, DH)
    mask_rows = lax.dynamic_slice_in_dim(
        block_mask, seq_index * (tok_rows // QBLK), tok_rows // QBLK, 0
    ).astype(jnp.float32)
    running_max = jnp.full((heads_dev, tok_rows), -1e30, jnp.float32)
    weighted = jnp.zeros((tok_rows, heads_dev, DH), jnp.float32)
    key_piece = gathered_by_axis(local_keys, SEQ, (1, 0, 2), 0)
    value_piece = gathered_by_axis(local_values, SEQ, (1, 0, 2), 0)
    row_count = key_piece.shape[0]
    position = jnp.arange(row_count, dtype=jnp.int32)
    source = position // shard_rows
    offset = position % shard_rows
    in_cache = offset < cache_rows
    cache_block = (source * cache_rows + offset) // CBLK
    onehot = (cache_block[:, None] == block_ids[None, :]).astype(jnp.float32)
    visible = jnp.dot(mask_rows, onehot.T, preferred_element_type=jnp.float32)
    allowed = jnp.where(in_cache[None, :], visible > 0.5, True)
    allowed = jnp.repeat(allowed, QBLK, axis=0)
    scores = (
        jnp.einsum(
            "qhd,khd->hqk",
            queries,
            key_piece.reshape(row_count, heads_dev, DH),
            preferred_element_type=jnp.float32,
        )
        * inv_root
    )
    masked = jnp.where(allowed[None], scores, -1e30)
    new_peak = jnp.maximum(running_max, jnp.max(masked, axis=2))
    raised = jnp.where(allowed[None], jnp.exp(scores - new_peak[:, :, None]), 0.0)
    rescale = jnp.exp(running_max - new_peak)
    totals = jnp.sum(raised, axis=2)
    weights = raised.astype(jnp.bfloat16)
    product = jnp.einsum(
        "hqk,khd->qhd",
        weights,
        value_piece.reshape(row_count, heads_dev, DH),
        preferred_element_type=jnp.float32,
    )
    weighted = weighted * rescale.T[:, :, None] + product
    running_max, totals, weighted = (new_peak, totals, weighted)
    result = weighted / totals.T[:, :, None]
    return result.reshape(tok_rows, width_dev).astype(jnp.bfloat16)


def solution(mesh):
    finer = Mesh(
        mesh.devices.reshape(8, 2, 2, mesh.shape["head"]), ("seq_0", "seq_1", "seq_2", "head")
    )
    return jax.shard_map(
        per_device,
        mesh=finer,
        in_specs=(
            P(SEQ, "head"),
            P(SEQ, "head"),
            P(SEQ, "head"),
            P(SEQ_HEAD, None),
            P(SEQ_HEAD, None),
            P(SEQ_HEAD, None),
            P(SEQ_HEAD, None),
            P(),
        ),
        out_specs=P(SEQ, "head"),
        check_vma=False,
    )
```

profile of v0, /device:TPU:1, one launch (start us, length us, event | category | flops | bytes accessed | tf_op | source)
XLA Modules:
  0.0 228.9 jit_solution(17435527228312048533)
XLA Ops:
  6.5 0.7 exponential_bitcast_fusion.1
  7.3 0.8 multiply_convert_fusion.1
  8.1 17.1 %all_to_all.38 = bf16[4,16,384]{2,0,1:T(4,128)(2,1)S(1)} all-to-all(bf16[4,16,384]{2,0,1:T(4,128)(2,1)S(1)} %bitcast.75), channel_id=1, replica_groups=mesh['seq_0'=8,'seq_1'=2,'seq_2'=2,'head'=16] {'head'}, dimensions={1} | all-to-all | bytes 98304 | tf_op jit(solution)/shard_map/all_to_all | solution.py:63
  25.3 0.9 pad_maximum_fusion
  26.2 9.4 %all-gather = bf16[384,384]{1,0:T(8,128)(2,1)} all-gather(bf16[192,384]{1,0:T(8,128)(2,1)S(1)} %pad_maximum_fusion), channel_id=2, replica_groups=mesh['seq_0'=8,'seq_1'=2,'seq_2'=2,'head'=16] {'seq_1'}, dimensions={0}, use_global_device_ids=true | all-gather | bytes 442368 | tf_op jit(solution)/shard_map/all_gather | solution.py:26
  35.7 0.7 exponential_bitcast_fusion
  36.4 0.8 multiply_convert_fusion
  37.2 13.7 %all_to_all.39 = bf16[4,16,384]{2,0,1:T(4,128)(2,1)S(1)} all-to-all(bf16[4,16,384]{2,0,1:T(4,128)(2,1)S(1)} %bitcast.76), channel_id=1, replica_groups=mesh['seq_0'=8,'seq_1'=2,'seq_2'=2,'head'=16] {'head'}, dimensions={1} | all-to-all | bytes 98304 | tf_op jit(solution)/shard_map/all_to_all | solution.py:66
  50.9 0.9 pad_maximum_fusion.1
  51.9 8.7 %all-gather.3 = bf16[384,384]{1,0:T(8,128)(2,1)} all-gather(bf16[192,384]{1,0:T(8,128)(2,1)S(1)} %pad_maximum_fusion.1), channel_id=5, replica_groups=mesh['seq_0'=8,'seq_1'=2,'seq_2'=2,'head'=16] {'seq_1'}, dimensions={0}, use_global_device_ids=true | all-gather | bytes 442368 | tf_op jit(solution)/shard_map/all_gather | solution.py:26
  60.6 17.8 %all-gather.11.cloned.1.call-done = bf16[16,192,384]{2,1,0:T(8,128)(2,1)} async-done(((bf16[2,192,384]{2,1,0:T(8,128)(2,1)}), bf16[16,192,384]{2,1,0:T(8,128)(2,1)}) %all-gather.11.cloned.1.call-update) | async-done | bytes 2359312 | tf_op jit(solution)/shard_map/all_gather | solution.py:26
  78.5 45.1 %all-gather.15.cloned.1.call-done = bf16[16,192,384]{2,1,0:T(8,128)(2,1)} async-done(((bf16[2,192,384]{2,1,0:T(8,128)(2,1)}), bf16[16,192,384]{2,1,0:T(8,128)(2,1)}) %all-gather.15.cloned.1.call-update) | async-done | bytes 2359312 | tf_op jit(solution)/shard_map/all_gather | solution.py:26
  123.7 1.0 fusion.5
  124.7 0.2 broadcast_in_dim.52
  124.9 1.4 copy.45
  126.4 25.9 %all-gather.13.cloned.1.call-done = bf16[16,2,192,384]{3,2,1,0:T(8,128)(2,1)} async-done(((bf16[8,2,192,384]{3,2,1,0:T(8,128)(2,1)}), bf16[16,2,192,384]{3,2,1,0:T(8,128)(2,1)}) %all-gather.13.cloned.1.call-update) | async-done | bytes 4718608 | tf_op jit(solution)/shard_map/all_gather | solution.py:26
  152.4 5.3 %copy.46 = bf16[8,2,2,192,384]{4,3,2,1,0:T(8,128)(2,1)} copy(bf16[8,2,2,192,384]{4,3,1,0,2:T(8,128)(2,1)} %bitcast.64) | data formatting | bytes 9437184 | tf_op jit(solution)/shard_map/transpose | solution.py:29
  157.6 13.0 %reshape_reshape_reshape.6 = bf16[6144,3,128]{2,1,0:T(4,128)(2,1)} reshape(bf16[8,2,2,192,384]{4,3,2,1,0:T(8,128)(2,1)} %copy.46) | data formatting | bytes 9437184 | tf_op jit(solution)/shard_map/reshape;reshape;reshape | solution.py:103
  170.6 9.3 %fusion = (f32[3,128]{1,0:T(4,128)S(1)}, f32[3,6144,128]{2,1,0:T(8,128)}) fusion(pred[128,6144]{0,1:T(8,128)(4,1)S(1)} %copy.45, bf16[128,3,128]{0,2,1:T(8,128)(2,1)S(1)} %bitcast.77, bf16[6144,3,128]{2,1,0:T(4,128)(2,1)} %reshape_reshape_reshape.6), kind=kOutput, calls=%fused_computation.2 | convolution fusion | flops 611057280 | bytes 15042048 | tf_op jit(solution)/shard_map/qhd,khd->hqk/dot_general | solution.py:100
  179.9 16.1 %copy.56 = bf16[8,2,2,192,384]{3,2,1,0,4:T(2,128)(2,1)} copy(bf16[8,2,2,192,384]{4,3,1,0,2:T(8,128)(2,1)} %bitcast.65) | data formatting | bytes 9437184 | tf_op jit(solution)/shard_map/reshape;reshape;reshape | solution.py:117
  196.0 13.7 %reshape.86 = bf16[6144,3,128]{0,2,1:T(8,128)(2,1)} reshape(bf16[8,2,2,192,384]{3,2,1,0,4:T(2,128)(2,1)} %copy.56) | data formatting | bytes 9437184 | tf_op jit(solution)/shard_map/reshape;reshape;reshape | solution.py:117
  209.7 5.6 %fusion.3 = f32[3,128]{1,0:T(4,128)S(1)} fusion(f32[3,6144,128]{2,1,0:T(8,128)} %get-tuple-element.8, f32[3,128]{1,0:T(4,128)S(1)} %get-tuple-element.6, pred[128,6144]{0,1:T(8,128)(4,1)S(1)} %copy.45), kind=kLoop, calls=%fused_computation.6 | loop fusion | flops 7077504 | bytes 10226688 | tf_op jit(solution)/shard_map/reduce_sum | solution.py:112
  215.3 6.3 %fusion.21 = bf16[128,3,128]{0,2,1:T(8,128)(2,1)S(1)} fusion(bf16[6144,3,128]{0,2,1:T(8,128)(2,1)S(1)} %bitcast.67, f32[3,6144,128]{2,1,0:T(8,128)} %get-tuple-element.8, f32[3,128]{1,0:T(4,128)S(1)} %get-tuple-element.6, pred[128,6144]{0,1:T(8,128)(4,1)S(1)} %copy.45, f32[128,3]{0,1:T(4,128)S(1)} %bitcast.79, f32[128,3]{0,1:T(4,128)S(1)} %get-tuple-element.5), kind=kOutput, calls=%fused_computation.19 | convolution fusion | flops 611205120 | bytes 15045120 | tf_op jit(solution)/shard_map/hqk,khd->qhd/dot_general | solution.py:114
  221.6 0.8 copy.53
  (24 shorter events, 0.6 us)
Async XLA Ops:
  6.5 119.7 %copy-start = (bf16[128,384]{1,0:T(8,128)(2,1)S(1)}, bf16[128,384]{1,0:T(8,128)(2,1)}, u32[]{:S(2)}) copy-start(bf16[128,384]{1,0:T(8,128)(2,1)} %param.8) | copy-start | bytes 294916
  6.5 71.9 %all-gather.11.cloned.1.call-start = ((), (), s32[]{:S(2)}) async-start(), calls=%async_computation.2 | async-start | bytes 2654208 | tf_op jit(solution)/shard_map/all_gather | solution.py:26
  35.6 87.9 %all-gather.15.cloned.1.call-start = ((), (), s32[]{:S(2)}) async-start(), calls=%async_computation.4 | async-start | bytes 2654208 | tf_op jit(solution)/shard_map/all_gather | solution.py:26
  60.6 91.8 %all-gather.13.cloned.1.call-start = ((), (), s32[]{:S(2)}) async-start(), calls=%async_computation.3 | async-start | bytes 7077888 | tf_op jit(solution)/shard_map/all_gather | solution.py:26
  78.5 101.4 %all-gather.17.cloned.1.call-start = ((), (), s32[]{:S(2)}) async-start(), calls=%async_computation.5 | async-start | bytes 7077888 | tf_op jit(solution)/shard_map/all_gather | solution.py:26
  209.7 5.6 %slice-start = ((s8[4718592]{0:T(1024)(128)(4,1)}), s8[4194304]{0:T(1024)(128)(4,1)S(1)}, s32[]{:S(2)}) async-start(s8[4718592]{0:T(1024)(128)(4,1)} %bitcast.66), calls=%async_computation.6 | async-start | bytes 8388608
  209.7 5.6 %slice-start.1 = ((s8[4718592]{0:T(1024)(128)(4,1)}), s8[524288]{0:T(1024)(128)(4,1)S(1)}, s32[]{:S(2)}) async-start(s8[4718592]{0:T(1024)(128)(4,1)} %bitcast.66), calls=%async_computation.7 | async-start | bytes 1048576
Sparse Core Ops, SparseCore 0:
  35.7 42.6 all-gather.10
  80.5 43.0 all-gather.14
  125.6 26.6 all-gather.12
  154.3 23.8 all-gather.16
where the time goes:
time: 230 us; the launch traced here: 229 us
  waiting for transfers between devices  88.9 us (39%)
  local copies, waits for them, and re-layouts  50.6 us (22%)
  blocking collectives  48.9 us (21%)
  matrix products  16.6 us (7%)
  between operations  13.2 us (6%)
  other arithmetic  10.5 us (5%)
    all_gather x4, waiting for transfers between devices, gather_in_order(): tiles = lax.all_gather(tiles, axes[k])  88.8 us
    another operation x2, local copies, waits for them, and re-layouts, per_device(): value_piece.reshape(row_count, heads_dev, DH)  29.8 us
    all_gather x2, blocking collectives, gather_in_order(): tiles = lax.all_gather(tiles, axes[k])  18.1 us
    all_to_all x1, blocking collectives, per_device(): lax.all_to_all(dequantize(cache_keys, key_exponent), 'head', split_axis=1...  17.1 us
    all_to_all x1, blocking collectives, per_device(): lax.all_to_all(dequantize(cache_values, value_exponent), 'head', split_ax...  13.7 us
    another operation x1, local copies, waits for them, and re-layouts, per_device(): key_piece.reshape(row_count, heads_dev, DH)  13 us
    dot_general x1, matrix products, per_device(): jnp.einsum('qhd,khd->hqk', queries, key_piece.reshape(row_count, heads_de...  9.27 us
    dot_general x1, matrix products, per_device(): jnp.einsum('hqk,khd->qhd', weights, value_piece.reshape(row_count, heads_...  6.31 us
  transfers between devices with their start and end apart: 4, of which 3 were waited for; matrix products, arithmetic and copies ran while one was open for 14% of the time, Pallas kernels for 0%

commit v1 on v0

v1 whole, which is shorter than its diff:
```python
import math

import jax
import jax.numpy as jnp
from jax import lax
from jax.experimental import pallas as pl
from jax.experimental.pallas import tpu as pltpu
from jax.sharding import PartitionSpec as P

DH = 128
QBLK = 64
CBLK = 32
SBLK = 4
HPD = 3
NY = 8
TOK = 128
CTOK = 64
MESH = pl.DeviceIdType.MESH
NEG = -1e30
SCALE = math.log2(math.e) / math.sqrt(DH)


def kernel(
    heads_n,
    seq_n,
    q_in,
    k_in,
    v_in,
    ck_in,
    cv_in,
    ke_in,
    ve_in,
    mask_in,
    o_ref,
    qb,
    kn,
    kc,
    dq,
    rc,
    stage,
    bias,
    acc,
    mx,
    sm,
    osend,
    orecv,
    ssend,
    srecv,
    loc_sem,
    a2a_s,
    a2a_r,
    q_s,
    q_r,
    n_s,
    n_r,
    nsib_s,
    nsib_r,
    c_s,
    c_r,
    csib_s,
    csib_r,
    o_s,
    o_r,
    st_s,
    st_r,
):
    seq = lax.axis_index("seq")
    head = lax.axis_index("head")
    y = seq // 4
    zh = (seq // 2) % 2
    core = seq % 2
    right = (lax.rem(seq + 4, seq_n), head)
    left = (lax.rem(seq + seq_n - 4, seq_n), head)
    zpart = (seq + 2 - 4 * zh, head)
    sib = (seq + 1 - 2 * core, head)

    local = []
    for h in range(HPD):
        cols = pl.ds(h * DH, DH)
        local.append(pltpu.make_async_copy(k_in.at[:, cols], kn.at[0, h, 0, 0:TOK], loc_sem.at[0, h]))
        local.append(pltpu.make_async_copy(v_in.at[:, cols], kn.at[0, h, 1, 0:TOK], loc_sem.at[1, h]))
    for h in range(HPD):
        cols = pl.ds(h * DH, DH)
        local.append(pltpu.make_async_copy(q_in.at[:, cols], qb.at[h, 0:TOK], loc_sem.at[2, h]))
    for cp in local:
        cp.start()

    barrier = pltpu.get_barrier_semaphore()
    for peer in (right, left, sib, zpart):
        pl.semaphore_signal(barrier, inc=1, device_id=peer, device_id_type=MESH)
    for r in range(1, heads_n):
        peer = (seq, lax.rem(head + r, heads_n))
        pl.semaphore_signal(barrier, inc=1, device_id=peer, device_id_type=MESH)

    for side, (c_in, e_in) in enumerate(((ck_in, ke_in), (cv_in, ve_in))):
        factor = jnp.exp2(e_in[...].astype(jnp.float32))
        for g in range(heads_n * HPD):
            cols = slice(g * DH, (g + 1) * DH)
            row = c_in[:, cols].astype(jnp.float32) * factor[:, g : g + 1]
            h = g % HPD
            dq[g // HPD, side, :, h * DH : (h + 1) * DH] = row.astype(jnp.bfloat16).astype(dq.dtype)

    mask = mask_in[...].astype(jnp.bfloat16)
    nq, nk = mask_in.shape
    qrow = lax.broadcasted_iota(jnp.int32, (2 * TOK, nq), 0)
    qcol = lax.broadcasted_iota(jnp.int32, (2 * TOK, nq), 1)
    zz = jnp.where(qrow < TOK, zh, 1 - zh)
    per = TOK // QBLK
    qblk = (y * 4 + zz * 2 + core) * per + (qrow & (TOK - 1)) // QBLK
    pick_q = jnp.where(qblk == qcol, 1.0, 0.0).astype(jnp.bfloat16)
    krow = lax.broadcasted_iota(jnp.int32, (nk, NY * 2 * CTOK), 0)
    kcol = lax.broadcasted_iota(jnp.int32, (nk, NY * 2 * CTOK), 1)
    rel = kcol // (2 * CTOK)
    other = (kcol // CTOK) & 1
    src_core = core + other * (1 - 2 * core)
    src = ((y + rel) & (NY - 1)) * 4 + zh * 2 + src_core
    kblk = src * (CTOK // CBLK) + (kcol & (CTOK - 1)) // CBLK
    pick_k = jnp.where(kblk == krow, 1.0, 0.0).astype(jnp.bfloat16)
    rows_mask = jnp.dot(pick_q, mask, preferred_element_type=jnp.float32).astype(jnp.bfloat16)
    seen = jnp.dot(rows_mask, pick_k, preferred_element_type=jnp.float32)
    bias[...] = jnp.where(seen > 0.5, 0.0, NEG)

    for cp in local:
        cp.wait()
    pl.semaphore_wait(barrier, 4 + heads_n - 1)

    def remote(src_ref, dst_ref, send, recv, peer):
        return pltpu.make_async_remote_copy(
            src_ref=src_ref, dst_ref=dst_ref, send_sem=send, recv_sem=recv, device_id=peer, device_id_type=MESH
        )

    def n_copy(src_rel, dst_rel, h, half, peer):
        if half is None:
            a, b, k = kn.at[src_rel, h, :, 0:TOK], kn.at[dst_rel, h, :, 0:TOK], 0
        else:
            a, b, k = kn.at[src_rel, h, half, 0:TOK], kn.at[dst_rel, h, half, 0:TOK], half
        return remote(a, b, n_s.at[dst_rel, h, k], n_r.at[dst_rel, h, k], peer)

    def n_sib(rel_y, h):
        return remote(
            kn.at[rel_y, h, :, 0:TOK], kn.at[rel_y, h, :, TOK : 2 * TOK], nsib_s.at[rel_y, h], nsib_r.at[rel_y, h], sib
        )

    def c_copy(src_rel, dst_rel, half, peer):
        if half is None:
            a, b, k = kc.at[src_rel, :, :, 0:CTOK], kc.at[dst_rel, :, :, 0:CTOK], 0
        else:
            a, b, k = kc.at[src_rel, :, half, 0:CTOK], kc.at[dst_rel, :, half, 0:CTOK], half
        return remote(a, b, c_s.at[dst_rel, k], c_r.at[dst_rel, k], peer)

    def c_sib(rel_y):
        return remote(
            kc.at[rel_y, :, :, 0:CTOK], kc.at[rel_y, :, :, CTOK : 2 * CTOK], csib_s.at[rel_y], csib_r.at[rel_y], sib
        )

    def q_copy(h):
        return remote(qb.at[h, 0:TOK], qb.at[h, TOK : 2 * TOK], q_s.at[h], q_r.at[h], zpart)

    def a2a_copy(r):
        dst = lax.rem(head + r, heads_n)
        return remote(dq.at[dst], rc.at[head], a2a_s.at[r], a2a_r.at[r], (seq, dst))

    def o_copy(h):
        return remote(osend.at[h], orecv.at[h], o_s.at[h], o_r.at[h], zpart)

    def st_copy(h):
        return remote(ssend.at[h], srecv.at[h], st_s.at[h], st_r.at[h], zpart)

    n_copy(0, 7, 0, None, right).start()
    n_copy(0, 1, 0, None, left).start()
    for r in range(1, heads_n):
        a2a_copy(r).start()
    for h in range(1, HPD):
        n_copy(0, 7, h, None, right).start()
        n_copy(0, 1, h, None, left).start()
    for h in range(HPD):
        q_copy(h).start()
    for h in range(HPD):
        n_sib(0, h).start()
    own = pltpu.make_async_copy(dq.at[head], rc.at[head], a2a_s.at[0])
    own.start()

    def attend(h, parts, first=False):
        q = qb[h]
        scores = []
        for keys, add in parts:
            s = lax.dot_general(q, keys[0], (((1,), (1,)), ((), ())), preferred_element_type=jnp.float32)
            if add is not None:
                s = s + add
            scores.append(s)
        top = None
        for s in scores:
            t = jnp.max(s, axis=1, keepdims=True)
            top = t if top is None else jnp.maximum(top, t)
        if not first:
            before = mx[h][:, 0:1]
            top = jnp.maximum(top, before)
        shift = top * SCALE
        total = None
        out = None
        for s, (keys, add) in zip(scores, parts):
            p = jnp.exp2(s * SCALE - shift)
            t = jnp.sum(p, axis=1, keepdims=True)
            o = jnp.dot(p.astype(jnp.bfloat16), keys[1], preferred_element_type=jnp.float32)
            total = t if total is None else total + t
            out = o if out is None else out + o
        if not first:
            back = jnp.exp2(before * SCALE - shift)
            total = sm[h][:, 0:1] * back + total
            out = acc[h] * back + out
        mx[h] = jnp.broadcast_to(top, (2 * TOK, DH))
        sm[h] = jnp.broadcast_to(total, (2 * TOK, DH))
        acc[h] = out

    def n_part(rel_y, h):
        return ((kn[rel_y, h, 0], kn[rel_y, h, 1]), None)

    def c_part(rel_y, h):
        return ((kc[rel_y, h, 0], kc[rel_y, h, 1]), bias[:, rel_y * 2 * CTOK : (rel_y + 1) * 2 * CTOK])

    def each_head(body):
        def step(h, carry):
            body(h)
            return carry

        lax.fori_loop(0, HPD, step, 0)

    def pass_n1(h):
        n_copy(0, 7, h, None, right).wait_recv()
        n_copy(7, 6, h, None, right).start()
        n_sib(7, h).start()
        n_copy(0, 1, h, None, left).wait_recv()
        n_copy(1, 2, h, None, left).start()
        n_sib(1, h).start()

    each_head(pass_n1)

    own.wait()
    for r in range(1, heads_n):
        a2a_copy(r).wait_recv()
    for side in range(2):
        for s in range(heads_n):
            stage[side, s * SBLK : (s + 1) * SBLK, :] = rc[s, side].astype(jnp.float32)
        for h in range(HPD):
            kc[0, h, side, 0:CTOK] = stage[side, :, h * DH : (h + 1) * DH].astype(jnp.bfloat16)

    def work0(h):
        n_sib(0, h).wait_recv()
        q_copy(h).wait_recv()
        attend(h, [n_part(0, h)], first=True)

    each_head(work0)

    c_copy(0, 7, None, right).start()
    c_copy(0, 1, None, left).start()
    c_sib(0).start()

    def work1(h):
        n_copy(7, 6, h, None, right).wait_recv()
        n_copy(6, 5, h, None, right).start()
        n_sib(6, h).start()
        n_copy(1, 2, h, None, left).wait_recv()
        n_copy(2, 3, h, None, left).start()
        n_sib(2, h).start()
        n_sib(7, h).wait_recv()
        n_sib(1, h).wait_recv()
        attend(h, [n_part(7, h), n_part(1, h)])

    each_head(work1)

    c_copy(0, 7, None, right).wait_recv()
    c_copy(7, 6, None, right).start()
    c_sib(7).start()
    c_copy(0, 1, None, left).wait_recv()
    c_copy(1, 2, None, left).start()
    c_sib(1).start()

    def work2(h):
        n_copy(6, 5, h, None, right).wait_recv()
        n_copy(5, 4, h, 0, right).start()
        n_sib(5, h).start()
        n_copy(2, 3, h, None, left).wait_recv()
        n_copy(3, 4, h, 1, left).start()
        n_sib(3, h).start()
        n_sib(6, h).wait_recv()
        n_sib(2, h).wait_recv()
        attend(h, [n_part(6, h), n_part(2, h)])

    each_head(work2)

    c_copy(7, 6, None, right).wait_recv()
    c_copy(6, 5, None, right).start()
    c_sib(6).start()
    c_copy(1, 2, None, left).wait_recv()
    c_copy(2, 3, None, left).start()
    c_sib(2).start()
    c_sib(0).wait_recv()
    c_sib(7).wait_recv()
    c_sib(1).wait_recv()

    def work3(h):
        n_copy(5, 4, h, 0, right).wait_recv()
        n_copy(3, 4, h, 1, left).wait_recv()
        n_sib(4, h).start()
        n_sib(5, h).wait_recv()
        n_sib(3, h).wait_recv()
        attend(h, [n_part(5, h), n_part(3, h), c_part(0, h)])

    each_head(work3)

    c_copy(6, 5, None, right).wait_recv()
    c_copy(5, 4, 0, right).start()
    c_sib(5).start()
    c_copy(2, 3, None, left).wait_recv()
    c_copy(3, 4, 1, left).start()
    c_sib(3).start()
    c_sib(6).wait_recv()
    c_sib(2).wait_recv()

    def work4(h):
        n_sib(4, h).wait_recv()
        attend(h, [n_part(4, h), c_part(7, h), c_part(1, h), c_part(6, h), c_part(2, h)])

    each_head(work4)

    c_copy(5, 4, 0, right).wait_recv()
    c_copy(3, 4, 1, left).wait_recv()
    c_sib(4).start()
    c_sib(5).wait_recv()
    c_sib(3).wait_recv()
    c_sib(4).wait_recv()

    def work5(h):
        attend(h, [c_part(5, h), c_part(3, h), c_part(4, h)])
        total = sm[h, TOK : 2 * TOK]
        osend[h] = (acc[h, TOK : 2 * TOK] / total).astype(osend.dtype)
        ssend[h, 0] = mx[h, TOK : 2 * TOK].T[0:8]
        ssend[h, 1] = total.T[0:8]
        o_copy(h).start()
        st_copy(h).start()

    each_head(work5)

    for h in range(HPD):
        o_copy(h).wait_recv()
        st_copy(h).wait_recv()
        m0 = mx[h, 0:TOK]
        l0 = sm[h, 0:TOK]
        m1 = jnp.concatenate([srecv[h, 0]] * (DH // 8), axis=0).T
        l1 = jnp.concatenate([srecv[h, 1]] * (DH // 8), axis=0).T
        m = jnp.maximum(m0, m1)
        w0 = jnp.exp2((m0 - m) * SCALE)
        w1 = jnp.exp2((m1 - m) * SCALE) * l1
        full = acc[h, 0:TOK] * w0 + orecv[h].astype(jnp.float32) * w1
        o_ref[:, h * DH : (h + 1) * DH] = (full / (l0 * w0 + w1)).astype(o_ref.dtype)

    for r in range(1, heads_n):
        a2a_copy(r).wait_send()

    def drain(h):
        n_copy(0, 7, h, None, right).wait_send()
        n_copy(7, 6, h, None, right).wait_send()
        n_copy(6, 5, h, None, right).wait_send()
        n_copy(5, 4, h, 0, right).wait_send()
        n_copy(0, 1, h, None, left).wait_send()
        n_copy(1, 2, h, None, left).wait_send()
        n_copy(2, 3, h, None, left).wait_send()
        n_copy(3, 4, h, 1, left).wait_send()
        for rel_y in range(NY):
            n_sib(rel_y, h).wait_send()
        q_copy(h).wait_send()
        o_copy(h).wait_send()
        st_copy(h).wait_send()

    each_head(drain)
    c_copy(0, 7, None, right).wait_send()
    c_copy(7, 6, None, right).wait_send()
    c_copy(6, 5, None, right).wait_send()
    c_copy(5, 4, 0, right).wait_send()
    c_copy(0, 1, None, left).wait_send()
    c_copy(1, 2, None, left).wait_send()
    c_copy(2, 3, None, left).wait_send()
    c_copy(3, 4, 1, left).wait_send()
    for rel_y in range(NY):
        c_sib(rel_y).wait_send()


def per_device(heads_n, seq_n, *args):
    import functools

    anywhere = pl.BlockSpec(memory_space=pl.ANY)
    vmem = pl.BlockSpec(memory_space=pltpu.VMEM)
    dma = pltpu.SemaphoreType.DMA
    f32, bf16 = jnp.float32, jnp.bfloat16
    return pl.pallas_call(
        functools.partial(kernel, heads_n, seq_n),
        out_shape=jax.ShapeDtypeStruct((TOK, HPD * DH), bf16),
        in_specs=[anywhere] * 3 + [vmem] * 5,
        out_specs=vmem,
        scratch_shapes=[
            pltpu.VMEM((HPD, 2 * TOK, DH), bf16),
            pltpu.VMEM((NY, HPD, 2, 2 * TOK, DH), bf16),
            pltpu.VMEM((NY, HPD, 2, 2 * CTOK, DH), bf16),
            pltpu.VMEM((heads_n, 2, SBLK, HPD * DH), bf16),
            pltpu.VMEM((heads_n, 2, SBLK, HPD * DH), bf16),
            pltpu.VMEM((2, CTOK, HPD * DH), f32),
            pltpu.VMEM((2 * TOK, NY * 2 * CTOK), f32),
            pltpu.VMEM((HPD, 2 * TOK, DH), f32),
            pltpu.VMEM((HPD, 2 * TOK, DH), f32),
            pltpu.VMEM((HPD, 2 * TOK, DH), f32),
            pltpu.VMEM((HPD, TOK, DH), bf16),
            pltpu.VMEM((HPD, TOK, DH), bf16),
            pltpu.VMEM((HPD, 2, 8, DH), f32),
            pltpu.VMEM((HPD, 2, 8, DH), f32),
            dma((3, HPD)),
            dma((heads_n,)),
            dma((heads_n,)),
            dma((HPD,)),
            dma((HPD,)),
            dma((NY, HPD, 2)),
            dma((NY, HPD, 2)),
            dma((NY, HPD)),
            dma((NY, HPD)),
            dma((NY, 2)),
            dma((NY, 2)),
            dma((NY,)),
            dma((NY,)),
            dma((HPD,)),
            dma((HPD,)),
            dma((HPD,)),
            dma((HPD,)),
        ],
        compiler_params=pltpu.CompilerParams(
            collective_id=0, has_side_effects=True, vmem_limit_bytes=60 * 1024 * 1024
        ),
        name="attend_ring",
    )(*args)


def solution(mesh):
    import functools

    both = P(("seq", "head"), None)
    own = P("seq", "head")
    return jax.shard_map(
        functools.partial(per_device, mesh.shape["head"], mesh.shape["seq"]),
        mesh=mesh,
        in_specs=(own, own, own, both, both, both, both, P()),
        out_specs=own,
        check_vma=False,
    )
```

time: 230 us -> 58 us (0.25)
  waiting for transfers between devices: 88.9 us -> 0 us
  Pallas kernels: 0 us -> 56.1 us
  local copies, waits for them, and re-layouts: 50.6 us -> 1.54 us
  blocking collectives: 48.9 us -> 0 us
  matrix products: 16.6 us -> 0 us
  between operations: 13.2 us -> 0.01 us
  other arithmetic: 10.5 us -> 0 us
    all_gather x4 -> x0, waiting for transfers between devices: 88.8 us -> none  [gather_in_order(): tiles = lax.all_gather(tiles, axes[k])]
    pallas_call x0 -> x1, Pallas kernels: none -> 56.1 us  [per_device(): pl.pallas_call(functools.partial(kernel, heads_n, seq_n), out_shape=jax.S...]
    another operation x3 -> x0, local copies, waits for them, and re-layouts: 42.7 us -> none  [the longest x2 29.8 us: per_device(): value_piece.reshape(row_count, heads_dev, DH)]
    all_to_all x2 -> x0, blocking collectives: 30.8 us -> none  [the longest x1 17.1 us: per_device(): lax.all_to_all(dequantize(cache_keys, key_exponent), 'head', split_axis=1...]
    all_gather x2 -> x0, blocking collectives: 18.1 us -> none  [gather_in_order(): tiles = lax.all_gather(tiles, axes[k])]
    dot_general x3 -> x0, matrix products: 16.6 us -> none  [the longest x1 9.27 us: per_device(): jnp.einsum('qhd,khd->hqk', queries, key_piece.reshape(row_count, heads_de...]
    reduce_sum x1 -> x0, other arithmetic: 5.57 us -> none  [per_device(): totals = jnp.sum(raised, axis=2)]
    transpose x1 -> x0, local copies, waits for them, and re-layouts: 5.26 us -> none  [gather_in_order(): tiles = tiles.transpose(*back, *range(len(axes), tiles.ndim))]
  transfers between devices with their start and end apart: 4 -> 0, of which waited for: 3 -> 0; matrix products, arithmetic and copies ran while one was open for 14% -> 0% of each run, Pallas kernels for 0% -> 0%
where the time goes in v1:
time: 58 us; the launch traced here: 57.7 us
  Pallas kernels  56.1 us (97%)
  local copies, waits for them, and re-layouts  1.54 us (3%)
    pallas_call x1, Pallas kernels, per_device(): pl.pallas_call(functools.partial(kernel, heads_n, seq_n), out_shape=jax.S...  56.1 us
    unnamed x1, local copies, waits for them, and re-layouts  1.54 us

profile of v1, /device:TPU:1, one launch (start us, length us, event | category | flops | bytes accessed | tf_op | source)
XLA Modules:
  0.0 57.7 jit_solution(6792859063038379619)
XLA Ops:
  0.0 56.1 %attend_ring.1 = bf16[128,384]{1,0:T(8,128)(2,1)} custom-call(bf16[128,384]{1,0:T(8,128)(2,1)} %q_in.1, bf16[128,384]{1,0:T(8,128)(2,1)} %k_in.1, bf16[128,384]{1,0:T(8,128)(2,1)} %v_in.1, bf16[4,6144]{1,0:T(4,128)(2,1)} %ck_in.1, bf16[4,6144]{1,0:T(4,128)(2,1)} %cv_in.1, s32[1,48]{1,0:T(1,128)} %ke_in.1, s32[1,48]{1,0:T(1,128)} %ve_in.1, s32[64,64]{1,0:T(8,128)} %mask_in.1), custom_call_target="tpu_custom_call" | custom-call | tf_op jit(solution)/shard_map/attend_ring/pallas_call | solution.py:395
  56.2 1.5 %copy.10 = bf16[128,384]{1,0:T(8,128)(2,1)} copy(bf16[128,384]{1,0:T(8,128)(2,1)} %attend_ring.1) | data formatting | bytes 196608

commit v2 on v1

v2 whole, which is shorter than its diff:
```python
import math

import jax
import jax.numpy as jnp
from jax import lax
from jax.experimental import pallas as pl
from jax.experimental.pallas import tpu as pltpu
from jax.sharding import PartitionSpec as P

DH = 128
QBLK = 64
CBLK = 32
SBLK = 4
HPD = 3
NY = 8
TOK = 128
CTOK = 64
MESH = pl.DeviceIdType.MESH
NEG = -1e30
SCALE = math.log2(math.e) / math.sqrt(DH)


def kernel(
    heads_n,
    seq_n,
    q_in,
    k_in,
    v_in,
    ck_in,
    cv_in,
    ke_in,
    ve_in,
    mask_in,
    o_ref,
    qb,
    kn,
    kc,
    dq,
    rc,
    stage,
    bias,
    acc,
    mx,
    sm,
    osend,
    orecv,
    ssend,
    srecv,
    ck,
    cv,
    ke,
    ve,
    mask_v,
    loc_sem,
    in_sem,
    in_kernel,
    a2a_s,
    a2a_r,
    q_s,
    q_r,
    n_s,
    n_r,
    nsib_s,
    nsib_r,
    c_s,
    c_r,
    csib_s,
    csib_r,
    o_s,
    o_r,
    st_s,
    st_r,
):
    seq = lax.axis_index("seq")
    head = lax.axis_index("head")
    y = seq // 4
    zh = (seq // 2) % 2
    core = seq % 2
    right = (lax.rem(seq + 4, seq_n), head)
    left = (lax.rem(seq + seq_n - 4, seq_n), head)
    zpart = (seq + 2 - 4 * zh, head)
    sib = (seq + 1 - 2 * core, head)

    local = []
    for h in range(HPD):
        cols = pl.ds(h * DH, DH)
        local.append(pltpu.make_async_copy(k_in.at[:, cols], kn.at[0, h, 0, 0:TOK], loc_sem.at[0, h]))
        local.append(pltpu.make_async_copy(v_in.at[:, cols], kn.at[0, h, 1, 0:TOK], loc_sem.at[1, h]))
    for h in range(HPD):
        cols = pl.ds(h * DH, DH)
        local.append(pltpu.make_async_copy(q_in.at[:, cols], qb.at[h, 0:TOK], loc_sem.at[2, h]))
    small = [
        pltpu.make_async_copy(a, b, in_sem.at[i])
        for i, (a, b) in enumerate(((ck_in, ck), (cv_in, cv), (ke_in, ke), (ve_in, ve), (mask_in, mask_v)))
    ]
    for cp in local + small:
        cp.start()

    barrier = pltpu.get_barrier_semaphore()
    for peer in (right, left, sib):
        pl.semaphore_signal(barrier, inc=1, device_id=peer, device_id_type=MESH)
    for r in range(1, heads_n):
        peer = (seq, lax.rem(head + r, heads_n))
        pl.semaphore_signal(barrier, inc=1, device_id=peer, device_id_type=MESH)


    @pl.when(zh == 0)
    def _():
        pl.semaphore_signal(barrier, inc=1, device_id=zpart, device_id_type=MESH)

    pl.semaphore_wait(barrier, 3 + heads_n - 1 + zh)

    def remote(src_ref, dst_ref, send, recv, peer):
        return pltpu.make_async_remote_copy(
            src_ref=src_ref, dst_ref=dst_ref, send_sem=send, recv_sem=recv, device_id=peer, device_id_type=MESH
        )

    def n_copy(src_rel, dst_rel, h, half, peer):
        if half is None:
            a, b, k = kn.at[src_rel, h, :, 0:TOK], kn.at[dst_rel, h, :, 0:TOK], 0
        else:
            a, b, k = kn.at[src_rel, h, half, 0:TOK], kn.at[dst_rel, h, half, 0:TOK], half
        return remote(a, b, n_s.at[dst_rel, h, k], n_r.at[dst_rel, h, k], peer)

    def n_sib(rel_y, h):
        return remote(
            kn.at[rel_y, h, :, 0:TOK], kn.at[rel_y, h, :, TOK : 2 * TOK], nsib_s.at[rel_y, h], nsib_r.at[rel_y, h], sib
        )

    def c_copy(src_rel, dst_rel, h, half, peer):
        if half is None:
            a, b, k = kc.at[src_rel, h, :, 0:CTOK], kc.at[dst_rel, h, :, 0:CTOK], 0
        else:
            a, b, k = kc.at[src_rel, h, half, 0:CTOK], kc.at[dst_rel, h, half, 0:CTOK], half
        return remote(a, b, c_s.at[dst_rel, h, k], c_r.at[dst_rel, h, k], peer)

    def c_sib(rel_y, h):
        return remote(
            kc.at[rel_y, h, :, 0:CTOK], kc.at[rel_y, h, :, CTOK : 2 * CTOK], csib_s.at[rel_y, h], csib_r.at[rel_y, h], sib
        )

    def q_copy(h):
        return remote(qb.at[h, 0:TOK], qb.at[h, TOK : 2 * TOK], q_s.at[h], q_r.at[h], zpart)

    def a2a_copy(r):
        dst = lax.rem(head + r, heads_n)
        return remote(dq.at[dst], rc.at[head], a2a_s.at[r], a2a_r.at[r], (seq, dst))

    def o_copy(h):
        return remote(osend.at[h], orecv.at[h], o_s.at[h], o_r.at[h], zpart)

    def st_copy(h):
        return remote(ssend.at[h], srecv.at[h], st_s.at[h], st_r.at[h], zpart)

    for h in range(HPD):
        for cp in (local[2 * h], local[2 * h + 1]):
            cp.wait()
        n_copy(0, 7, h, None, right).start()
        n_copy(0, 1, h, None, left).start()
    for h in range(HPD):
        local[2 * HPD + h].wait()

    @pl.when(zh == 1)
    def _():
        pl.semaphore_signal(in_kernel, inc=1, device_id=zpart, device_id_type=MESH)
        for h in range(HPD):
            q_copy(h).start()

    for cp in small[:4]:
        cp.wait()
    for side, (c_in, e_in) in enumerate(((ck, ke), (cv, ve))):
        factor = jnp.exp2(e_in[...].astype(jnp.float32))
        for g in range(heads_n * HPD):
            cols = slice(g * DH, (g + 1) * DH)
            row = c_in[:, cols].astype(jnp.float32) * factor[:, g : g + 1]
            h = g % HPD
            dq[g // HPD, side, :, h * DH : (h + 1) * DH] = row.astype(jnp.bfloat16).astype(dq.dtype)

    for r in range(1, heads_n):
        a2a_copy(r).start()
    own = pltpu.make_async_copy(dq.at[head], rc.at[head], a2a_s.at[0])
    own.start()
    for h in range(HPD):
        n_sib(0, h).start()
    small[4].wait()
    mask = mask_v[...].astype(jnp.bfloat16)
    nq, nk = mask_v.shape
    qrow = lax.broadcasted_iota(jnp.int32, (2 * TOK, nq), 0)
    qcol = lax.broadcasted_iota(jnp.int32, (2 * TOK, nq), 1)
    zz = jnp.where(qrow < TOK, zh, 1 - zh)
    per = TOK // QBLK
    qblk = (y * 4 + zz * 2 + core) * per + (qrow & (TOK - 1)) // QBLK
    pick_q = jnp.where(qblk == qcol, 1.0, 0.0).astype(jnp.bfloat16)
    krow = lax.broadcasted_iota(jnp.int32, (nk, NY * 2 * CTOK), 0)
    kcol = lax.broadcasted_iota(jnp.int32, (nk, NY * 2 * CTOK), 1)
    rel = kcol // (2 * CTOK)
    other = (kcol // CTOK) & 1
    src_core = core + other * (1 - 2 * core)
    src = ((y + rel) & (NY - 1)) * 4 + zh * 2 + src_core
    kblk = src * (CTOK // CBLK) + (kcol & (CTOK - 1)) // CBLK
    pick_k = jnp.where(kblk == krow, 1.0, 0.0).astype(jnp.bfloat16)
    rows_mask = jnp.dot(pick_q, mask, preferred_element_type=jnp.float32).astype(jnp.bfloat16)
    seen = jnp.dot(rows_mask, pick_k, preferred_element_type=jnp.float32)
    bias[...] = jnp.where(seen > 0.5, 0.0, NEG)

    def attend(h, parts, rows=slice(0, 2 * TOK), first=False):
        q = qb[h, rows]
        scores = []
        for keys, add in parts:
            s = lax.dot_general(q, keys[0], (((1,), (1,)), ((), ())), preferred_element_type=jnp.float32)
            if add is not None:
                s = s + add[rows]
            scores.append(s)
        top = None
        for s in scores:
            t = jnp.max(s, axis=1, keepdims=True)
            top = t if top is None else jnp.maximum(top, t)
        if not first:
            before = mx[h, rows][:, 0:1]
            top = jnp.maximum(top, before)
        shift = top * SCALE
        total = None
        out = None
        for s, (keys, add) in zip(scores, parts):
            p = jnp.exp2(s * SCALE - shift)
            t = jnp.sum(p, axis=1, keepdims=True)
            o = jnp.dot(p.astype(jnp.bfloat16), keys[1], preferred_element_type=jnp.float32)
            total = t if total is None else total + t
            out = o if out is None else out + o
        if not first:
            back = jnp.exp2(before * SCALE - shift)
            total = sm[h, rows][:, 0:1] * back + total
            out = acc[h, rows] * back + out
        mx[h, rows] = jnp.broadcast_to(top, out.shape)
        sm[h, rows] = jnp.broadcast_to(total, out.shape)
        acc[h, rows] = out

    def n_part(rel_y, h):
        return ((kn[rel_y, h, 0], kn[rel_y, h, 1]), None)

    def c_part(rel_y, h):
        return ((kc[rel_y, h, 0], kc[rel_y, h, 1]), bias.at[:, rel_y * 2 * CTOK : (rel_y + 1) * 2 * CTOK])

    def relay(copy, to_sib, d, h):
        back_r = 8 - d + 1 if d > 1 else 0
        copy(back_r, 8 - d, h, None, right).wait_recv()
        if d < 3:
            copy(8 - d, 7 - d, h, None, right).start()
        else:
            copy(5, 4, h, 0, right).start()
        to_sib(8 - d, h).start()
        copy(d - 1, d, h, None, left).wait_recv()
        if d < 3:
            copy(d, d + 1, h, None, left).start()
        else:
            copy(3, 4, h, 1, left).start()
        to_sib(d, h).start()

    def last(h):
        for copy, to_sib in ((n_copy, n_sib), (c_copy, c_sib)):
            copy(5, 4, h, 0, right).wait_recv()
            copy(3, 4, h, 1, left).wait_recv()
            to_sib(4, h).start()

    def need(h, new=(), cached=()):
        for rel_y in new:
            n_sib(rel_y, h).wait_recv()
        for rel_y in cached:
            c_sib(rel_y, h).wait_recv()

    for h in range(HPD):
        relay(n_copy, n_sib, 1, h)

    own.wait()
    for r in range(1, heads_n):
        a2a_copy(r).wait_recv()
    for side in range(2):
        for s in range(heads_n):
            stage[side, s * SBLK : (s + 1) * SBLK, :] = rc[s, side].astype(jnp.float32)
    for h in range(HPD):
        for side in range(2):
            kc[0, h, side, 0:CTOK] = stage[side, :, h * DH : (h + 1) * DH].astype(jnp.bfloat16)
    relay(n_copy, n_sib, 2, 0)
    for h in range(HPD):
        c_copy(0, 7, h, None, right).start()
        c_copy(0, 1, h, None, left).start()
        c_sib(0, h).start()

    mine, theirs = slice(0, TOK), slice(TOK, 2 * TOK)

    def work_a(h, rows):
        attend(h, [n_part(0, h), n_part(7, h), n_part(1, h)], rows=rows, first=True)

    def work_b(h):
        need(h, new=(6, 2), cached=(0, 7, 1))
        attend(h, [n_part(6, h), n_part(2, h), c_part(0, h), c_part(7, h), c_part(1, h)])

    def work_d(h):
        need(h, new=(5, 3), cached=(6, 2))
        attend(h, [n_part(5, h), n_part(3, h), c_part(6, h), c_part(2, h)])

    def work_f(h):
        need(h, cached=(5, 3))
        attend(h, [c_part(5, h), c_part(3, h)])

    def work_g(h):
        need(h, new=(4,), cached=(4,))
        attend(h, [n_part(4, h), c_part(4, h)], rows=theirs)
        total = sm[h, theirs]
        osend[h] = (acc[h, theirs] / total).astype(osend.dtype)
        ssend[h, 0:1] = mx[h, theirs].T[0:1]
        ssend[h, 1:2] = total.T[0:1]
        o_copy(h).start()
        st_copy(h).start()

    @pl.when(zh == 0)
    def _():
        pl.semaphore_wait(in_kernel, 1)
        for h in range(HPD):
            q_copy(h).start()

    for h in range(HPD):
        need(h, new=(0, 7, 1))
        work_a(h, mine)
    for h in range(HPD):
        relay(c_copy, c_sib, 1, h)
    relay(n_copy, n_sib, 2, 1)
    relay(n_copy, n_sib, 2, 2)
    for h in range(HPD):
        q_copy(h).wait_recv()
        work_a(h, theirs)
    for h in range(HPD):
        relay(c_copy, c_sib, 2, h)
    relay(n_copy, n_sib, 3, 0)
    work_b(0)
    work_d(0)
    work_b(1)
    relay(c_copy, c_sib, 3, 0)
    relay(n_copy, n_sib, 3, 1)
    relay(c_copy, c_sib, 3, 1)
    relay(n_copy, n_sib, 3, 2)
    relay(c_copy, c_sib, 3, 2)
    work_b(2)
    work_d(1)
    work_f(0)
    last(0)
    work_d(2)
    work_f(1)
    last(1)
    work_f(2)
    work_g(0)
    last(2)
    work_g(1)
    work_g(2)
    for h in range(HPD):
        attend(h, [n_part(4, h), c_part(4, h)], rows=mine)

    for h in range(HPD):
        o_copy(h).wait_recv()
        st_copy(h).wait_recv()
        m0 = mx[h, 0:TOK]
        l0 = sm[h, 0:TOK]
        m1 = jnp.broadcast_to(srecv[h, 0:1], (TOK, DH)).T
        l1 = jnp.broadcast_to(srecv[h, 1:2], (TOK, DH)).T
        m = jnp.maximum(m0, m1)
        w0 = jnp.exp2((m0 - m) * SCALE)
        w1 = jnp.exp2((m1 - m) * SCALE) * l1
        full = acc[h, 0:TOK] * w0 + orecv[h].astype(jnp.float32) * w1
        o_ref[:, h * DH : (h + 1) * DH] = (full / (l0 * w0 + w1)).astype(o_ref.dtype)

    for r in range(1, heads_n):
        a2a_copy(r).wait_send()
    for h in range(HPD):
        for copy, to_sib in ((n_copy, n_sib), (c_copy, c_sib)):
            for d in range(3):
                copy(8 - d if d else 0, 7 - d, h, None, right).wait_send()
                copy(d, d + 1, h, None, left).wait_send()
            copy(5, 4, h, 0, right).wait_send()
            copy(3, 4, h, 1, left).wait_send()
            for rel_y in range(NY):
                to_sib(rel_y, h).wait_send()
        q_copy(h).wait_send()
        o_copy(h).wait_send()
        st_copy(h).wait_send()


def per_device(heads_n, seq_n, *args):
    import functools

    hbm = pl.BlockSpec(memory_space=pltpu.HBM)
    vmem = pl.BlockSpec(memory_space=pltpu.VMEM)
    dma = pltpu.SemaphoreType.DMA
    f32, bf16 = jnp.float32, jnp.bfloat16
    return pl.pallas_call(
        functools.partial(kernel, heads_n, seq_n),
        out_shape=jax.ShapeDtypeStruct((TOK, HPD * DH), bf16),
        in_specs=[hbm] * 8,
        out_specs=vmem,
        scratch_shapes=[
            pltpu.VMEM((HPD, 2 * TOK, DH), bf16),
            pltpu.VMEM((NY, HPD, 2, 2 * TOK, DH), bf16),
            pltpu.VMEM((NY, HPD, 2, 2 * CTOK, DH), bf16),
            pltpu.VMEM((heads_n, 2, SBLK, HPD * DH), bf16),
            pltpu.VMEM((heads_n, 2, SBLK, HPD * DH), bf16),
            pltpu.VMEM((2, CTOK, HPD * DH), f32),
            pltpu.VMEM((2 * TOK, NY * 2 * CTOK), f32),
            pltpu.VMEM((HPD, 2 * TOK, DH), f32),
            pltpu.VMEM((HPD, 2 * TOK, DH), f32),
            pltpu.VMEM((HPD, 2 * TOK, DH), f32),
            pltpu.VMEM((HPD, TOK, DH), bf16),
            pltpu.VMEM((HPD, TOK, DH), bf16),
            pltpu.VMEM((HPD, 2, DH), f32),
            pltpu.VMEM((HPD, 2, DH), f32),
            pltpu.VMEM((SBLK, heads_n * HPD * DH), bf16),
            pltpu.VMEM((SBLK, heads_n * HPD * DH), bf16),
            pltpu.VMEM((1, heads_n * HPD), jnp.int32),
            pltpu.VMEM((1, heads_n * HPD), jnp.int32),
            pltpu.VMEM(args[7].shape, jnp.int32),
            dma((3, HPD)),
            dma((5,)),
            pltpu.SemaphoreType.REGULAR,
            dma((heads_n,)),
            dma((heads_n,)),
            dma((HPD,)),
            dma((HPD,)),
            dma((NY, HPD, 2)),
            dma((NY, HPD, 2)),
            dma((NY, HPD)),
            dma((NY, HPD)),
            dma((NY, HPD, 2)),
            dma((NY, HPD, 2)),
            dma((NY, HPD)),
            dma((NY, HPD)),
            dma((HPD,)),
            dma((HPD,)),
            dma((HPD,)),
            dma((HPD,)),
        ],
        compiler_params=pltpu.CompilerParams(
            collective_id=0, has_side_effects=True, vmem_limit_bytes=60 * 1024 * 1024
        ),
        name="attend_ring",
    )(*args)


def solution(mesh):
    import functools

    both = P(("seq", "head"), None)
    own = P("seq", "head")
    return jax.shard_map(
        functools.partial(per_device, mesh.shape["head"], mesh.shape["seq"]),
        mesh=mesh,
        in_specs=(own, own, own, both, both, both, both, P()),
        out_specs=own,
        check_vma=False,
    )
```

time: 58 us -> 54.9 us (0.947)
  Pallas kernels: 56.1 us -> 53.2 us
    pallas_call x1, Pallas kernels: 56.1 us -> 53.2 us  [per_device(): pl.pallas_call(functools.partial(kernel, heads_n, seq_n), out_shape=jax.S...]
where the time goes in v2:
time: 54.9 us; the launch traced here: 54.8 us
  Pallas kernels  53.2 us (97%)
  local copies, waits for them, and re-layouts  1.54 us (3%)
    pallas_call x1, Pallas kernels, per_device(): pl.pallas_call(functools.partial(kernel, heads_n, seq_n), out_shape=jax.S...  53.2 us
    unnamed x1, local copies, waits for them, and re-layouts  1.54 us

profile of v2, /device:TPU:1, one launch (start us, length us, event | category | flops | bytes accessed | tf_op | source)
XLA Modules:
  0.0 54.8 jit_solution(4285748400973004224)
XLA Ops:
  0.0 53.2 %attend_ring.1 = bf16[128,384]{1,0:T(8,128)(2,1)} custom-call(bf16[128,384]{1,0:T(8,128)(2,1)} %q_in.1, bf16[128,384]{1,0:T(8,128)(2,1)} %k_in.1, bf16[128,384]{1,0:T(8,128)(2,1)} %v_in.1, bf16[4,6144]{1,0:T(4,128)(2,1)} %ck_in.1, bf16[4,6144]{1,0:T(4,128)(2,1)} %cv_in.1, s32[1,48]{1,0:T(1,128)} %ke_in.1, s32[1,48]{1,0:T(1,128)} %ve_in.1, s32[64,64]{1,0:T(8,128)} %mask_in.1), custom_call_target="tpu_custom_call" | custom-call | tf_op jit(solution)/shard_map/attend_ring/pallas_call | solution.py:394
  53.2 1.5 %copy.10 = bf16[128,384]{1,0:T(8,128)(2,1)} copy(bf16[128,384]{1,0:T(8,128)(2,1)} %attend_ring.1) | data formatting | bytes 196608

commit v3 on v2

v3 whole, which is shorter than its diff:
```python
import math

import jax
import jax.numpy as jnp
from jax import lax
from jax.experimental import pallas as pl
from jax.experimental.pallas import tpu as pltpu
from jax.sharding import PartitionSpec as P

DH = 128
QBLK = 64
CBLK = 32
SBLK = 4
HPD = 3
NY = 8
ZLO = 4
TOK = 128
CTOK = 64
MESH = pl.DeviceIdType.MESH
NEG = -1e30
SCALE = math.log2(math.e) / math.sqrt(DH)


def kernel(
    heads_n,
    seq_n,
    q_in,
    k_in,
    v_in,
    ck_in,
    cv_in,
    ke_in,
    ve_in,
    mask_in,
    o_ref,
    qb,
    kn,
    dq,
    rc,
    stage,
    bias,
    acc,
    mx,
    sm,
    osend,
    orecv,
    ssend,
    srecv,
    ck,
    cv,
    ke,
    ve,
    mask_v,
    loc_sem,
    in_sem,
    in_kernel,
    in_peers,
    a2a_s,
    a2a_r,
    q_s,
    q_r,
    n_s,
    n_r,
    nsib_s,
    nsib_r,
    o_s,
    o_r,
    st_s,
    st_r,
):
    seq = lax.axis_index("seq")
    head = lax.axis_index("head")
    y = seq // 4
    zh = (seq // 2) % 2
    core = seq % 2
    right = (lax.rem(seq + 4, seq_n), head)
    left = (lax.rem(seq + seq_n - 4, seq_n), head)
    zpart = (seq + 2 - 4 * zh, head)
    sib = (seq + 1 - 2 * core, head)

    local = []
    for h in range(HPD):
        cols = pl.ds(h * DH, DH)
        local.append(pltpu.make_async_copy(k_in.at[:, cols], kn.at[0, h, 0, 0:TOK], loc_sem.at[0, h]))
        local.append(pltpu.make_async_copy(v_in.at[:, cols], kn.at[0, h, 1, 0:TOK], loc_sem.at[1, h]))
    for h in range(HPD):
        cols = pl.ds(h * DH, DH)
        local.append(pltpu.make_async_copy(q_in.at[:, cols], qb.at[h, 0:TOK], loc_sem.at[2, h]))
    small = [
        pltpu.make_async_copy(a, b, in_sem.at[i])
        for i, (a, b) in enumerate(((ck_in, ck), (cv_in, cv), (ke_in, ke), (ve_in, ve), (mask_in, mask_v)))
    ]
    for cp in local + small:
        cp.start()

    first_half, second_half = zh == 0, zh == 1
    zl = lax.rem(head, ZLO)
    peers = [lax.rem(head + r, heads_n) for r in range(heads_n)]
    barrier = pltpu.get_barrier_semaphore()
    for peer in (right, left, sib):
        pl.semaphore_signal(barrier, inc=1, device_id=peer, device_id_type=MESH)

    @pl.when(first_half)
    def _():
        for p in peers[1:]:

            @pl.when(lax.rem(p, ZLO) >= zl)
            def _():
                pl.semaphore_signal(barrier, inc=1, device_id=(seq, p), device_id_type=MESH)

        for p in peers:
            pl.semaphore_signal(barrier, inc=1, device_id=(zpart[0], p), device_id_type=MESH)

    def dequantize():
        for cp in small[:4]:
            cp.wait()
        for side, (c_in, e_in) in enumerate(((ck, ke), (cv, ve))):
            factor = jnp.exp2(e_in[...].astype(jnp.float32))
            for g in range(heads_n * HPD):
                cols = slice(g * DH, (g + 1) * DH)
                row = c_in[:, cols].astype(jnp.float32) * factor[:, g : g + 1]
                h = g % HPD
                dq[g // HPD, side, :, h * DH : (h + 1) * DH] = row.astype(jnp.bfloat16).astype(dq.dtype)

    @pl.when(second_half)
    def _():
        dequantize()

    level = heads_n // ZLO
    pl.semaphore_wait(barrier, 3 + (1 - zh) * (level * (zl + 1) - 1) + zh * heads_n)

    def remote(src_ref, dst_ref, send, recv, peer):
        return pltpu.make_async_remote_copy(
            src_ref=src_ref, dst_ref=dst_ref, send_sem=send, recv_sem=recv, device_id=peer, device_id_type=MESH
        )

    def n_copy(src_rel, dst_rel, h, half, peer):
        if half is None:
            a, b, k = kn.at[src_rel, h, :, 0:TOK], kn.at[dst_rel, h, :, 0:TOK], 0
        else:
            a, b, k = kn.at[src_rel, h, half, 0:TOK], kn.at[dst_rel, h, half, 0:TOK], half
        return remote(a, b, n_s.at[dst_rel, h, k], n_r.at[dst_rel, h, k], peer)

    def n_sib(rel_y, h):
        return remote(
            kn.at[rel_y, h, :, 0:TOK], kn.at[rel_y, h, :, TOK : 2 * TOK], nsib_s.at[rel_y, h], nsib_r.at[rel_y, h], sib
        )

    def q_copy(h):
        return remote(qb.at[h, 0:TOK], qb.at[h, TOK : 2 * TOK], q_s.at[h], q_r.at[h], zpart)

    def a2a_near(r):
        return remote(dq.at[peers[r]], rc.at[0, head], a2a_s.at[r], a2a_r.at[0, r], (seq, peers[r]))

    def a2a_far(r):
        return remote(dq.at[peers[r]], rc.at[1, head], a2a_s.at[r], a2a_r.at[1, r], (zpart[0], peers[r]))

    def o_copy(h):
        return remote(osend.at[h], orecv.at[h], o_s.at[h], o_r.at[h], zpart)

    def st_copy(h):
        return remote(ssend.at[h], srecv.at[h], st_s.at[h], st_r.at[h], zpart)

    @pl.when(second_half)
    def _():
        for r in range(heads_n):
            a2a_far(r).start()

    for h in range(HPD):
        for cp in (local[2 * h], local[2 * h + 1]):
            cp.wait()
        n_copy(0, 7, h, None, right).start()
        n_copy(0, 1, h, None, left).start()
    for h in range(HPD):
        n_sib(0, h).start()
    for h in range(HPD):
        local[2 * HPD + h].wait()

    @pl.when(second_half)
    def _():
        pl.semaphore_signal(in_kernel, inc=1, device_id=zpart, device_id_type=MESH)
        for h in range(HPD):
            q_copy(h).start()

    @pl.when(first_half)
    def _():
        for p in peers[1:]:

            @pl.when(lax.rem(p, ZLO) < zl)
            def _():
                pl.semaphore_signal(in_peers, inc=1, device_id=(seq, p), device_id_type=MESH)

    small[4].wait()

    @pl.when(first_half)
    def _():
        dequantize()

    def attend(h, parts, rows=slice(0, 2 * TOK), first=False):
        q = qb[h, rows]
        scores = []
        for keys, add in parts:
            s = lax.dot_general(q, keys[0], (((1,), (1,)), ((), ())), preferred_element_type=jnp.float32)
            if add is not None:
                s = s + add[rows]
            scores.append(s)
        top = None
        for s in scores:
            t = jnp.max(s, axis=1, keepdims=True)
            top = t if top is None else jnp.maximum(top, t)
        if not first:
            before = mx[h, rows][:, 0:1]
            top = jnp.maximum(top, before)
        shift = top * SCALE
        total = None
        out = None
        for s, (keys, add) in zip(scores, parts):
            p = jnp.exp2(s * SCALE - shift)
            t = jnp.sum(p, axis=1, keepdims=True)
            o = jnp.dot(p.astype(jnp.bfloat16), keys[1], preferred_element_type=jnp.float32)
            total = t if total is None else total + t
            out = o if out is None else out + o
        if not first:
            back = jnp.exp2(before * SCALE - shift)
            total = sm[h, rows][:, 0:1] * back + total
            out = acc[h, rows] * back + out
        mx[h, rows] = jnp.broadcast_to(top, out.shape)
        sm[h, rows] = jnp.broadcast_to(total, out.shape)
        acc[h, rows] = out

    def n_part(rel_y, h):
        return ((kn[rel_y, h, 0], kn[rel_y, h, 1]), None)

    def c_part(rel_y, h):
        return (
            (kn[rel_y, HPD + h, 0], kn[rel_y, HPD + h, 1]),
            bias.at[:, rel_y * 4 * CTOK : (rel_y + 1) * 4 * CTOK],
        )

    def relay(d, h):
        back_r = 8 - d + 1 if d > 1 else 0
        n_copy(back_r, 8 - d, h, None, right).wait_recv()
        if d < 3:
            n_copy(8 - d, 7 - d, h, None, right).start()
        else:
            n_copy(5, 4, h, 0, right).start()
        n_sib(8 - d, h).start()
        n_copy(d - 1, d, h, None, left).wait_recv()
        if d < 3:
            n_copy(d, d + 1, h, None, left).start()
        else:
            n_copy(3, 4, h, 1, left).start()
        n_sib(d, h).start()

    def last(h):
        n_copy(5, 4, h, 0, right).wait_recv()
        n_copy(3, 4, h, 1, left).wait_recv()
        n_sib(4, h).start()

    def need(h, rels):
        for rel_y in rels:
            n_sib(rel_y, h).wait_recv()

    every, mine, theirs = slice(0, 2 * TOK), slice(0, TOK), slice(TOK, 2 * TOK)

    def new_work(h, rels, rows=every, first=False):
        attend(h, [n_part(rel_y, h) for rel_y in rels], rows=rows, first=first)

    def cached_work(h, rels, rows=every):
        attend(h, [c_part(rel_y, h) for rel_y in rels], rows=rows)

    def share(h):
        total = sm[h, theirs]
        osend[h] = (acc[h, theirs] / total).astype(osend.dtype)
        ssend[h, 0:1] = mx[h, theirs].T[0:1]
        ssend[h, 1:2] = total.T[0:1]
        o_copy(h).start()
        st_copy(h).start()

    for h in range(HPD):
        relay(1, h)

    @pl.when(first_half)
    def _():

        @pl.when(zl < ZLO - 1)
        def _():
            pl.semaphore_wait(in_peers, level * (ZLO - 1 - zl))

        for r in range(1, heads_n):
            a2a_near(r).start()
        pltpu.make_async_copy(dq.at[head], rc.at[0, head], a2a_s.at[0]).start()

    relay(2, 0)

    @pl.when(first_half)
    def _():
        mask = mask_v[...].astype(jnp.bfloat16)
        nq, nk = mask_v.shape
        qrow = lax.broadcasted_iota(jnp.int32, (2 * TOK, nq), 0)
        qcol = lax.broadcasted_iota(jnp.int32, (2 * TOK, nq), 1)
        zz = jnp.where(qrow < TOK, zh, 1 - zh)
        per = TOK // QBLK
        qblk = (y * 4 + zz * 2 + core) * per + (qrow & (TOK - 1)) // QBLK
        pick_q = jnp.where(qblk == qcol, 1.0, 0.0).astype(jnp.bfloat16)
        krow = lax.broadcasted_iota(jnp.int32, (nk, NY * 4 * CTOK), 0)
        kcol = lax.broadcasted_iota(jnp.int32, (nk, NY * 4 * CTOK), 1)
        rel = kcol // (4 * CTOK)
        other = (kcol // (2 * CTOK)) & 1
        src_core = core + other * (1 - 2 * core)
        src = ((y + rel) & (NY - 1)) * 4 + ((kcol // CTOK) & 1) * 2 + src_core
        kblk = src * (CTOK // CBLK) + (kcol & (CTOK - 1)) // CBLK
        pick_k = jnp.where(kblk == krow, 1.0, 0.0).astype(jnp.bfloat16)
        rows_mask = jnp.dot(pick_q, mask, preferred_element_type=jnp.float32).astype(jnp.bfloat16)
        seen = jnp.dot(rows_mask, pick_k, preferred_element_type=jnp.float32)
        bias[...] = jnp.where(seen > 0.5, 0.0, NEG)

    relay(2, 1)
    relay(2, 2)

    for h in range(HPD):
        need(h, (0, 7, 1))
        new_work(h, (0, 7, 1), rows=mine, first=True)
    for h in range(HPD):
        relay(3, h)

    @pl.when(first_half)
    def _():
        pltpu.make_async_copy(dq.at[head], rc.at[0, head], a2a_s.at[0]).wait()
        for r in range(1, heads_n):
            a2a_near(r).wait_recv()
        for r in range(heads_n):
            a2a_far(r).wait_recv()
        for side in range(2):
            for half in range(2):
                for src in range(heads_n):
                    row = half * CTOK + src * SBLK
                    stage[side, row : row + SBLK, :] = rc[half, src, side].astype(jnp.float32)
        for h in range(HPD):
            for side in range(2):
                kn[0, HPD + h, side, 0:TOK] = stage[side, :, h * DH : (h + 1) * DH].astype(jnp.bfloat16)
        for h in range(HPD, 2 * HPD):
            n_copy(0, 7, h, None, right).start()
            n_copy(0, 1, h, None, left).start()
            n_sib(0, h).start()

    @pl.when(first_half)
    def _():
        pl.semaphore_wait(in_kernel, 1)
        for h in range(HPD):
            q_copy(h).start()

    for h in range(HPD):
        last(h)
    for h in range(HPD):
        q_copy(h).wait_recv()
        new_work(h, (0, 7, 1), rows=theirs, first=True)

    @pl.when(second_half)
    def _():
        for h in range(HPD):
            need(h, (6, 2, 5, 3))
            new_work(h, (6, 2, 5, 3))
            need(h, (4,))
            new_work(h, (4,))
            share(h)

    @pl.when(first_half)
    def _():
        for h in range(HPD):
            relay(1, HPD + h)
            need(h, (6, 2, 5, 3))
            new_work(h, (6, 2, 5, 3))
        relay(2, HPD)
        for h in range(HPD):
            need(h, (4,))
            new_work(h, (4,))
        relay(2, HPD + 1)
        need(HPD, (0, 7, 1))
        cached_work(0, (0, 7, 1))
        relay(2, HPD + 2)
        need(HPD + 1, (0, 7, 1))
        cached_work(1, (0, 7, 1))
        relay(3, HPD)
        need(HPD + 2, (0, 7, 1))
        cached_work(2, (0, 7, 1))
        relay(3, HPD + 1)
        need(HPD, (6, 2))
        cached_work(0, (6, 2))
        relay(3, HPD + 2)
        for h in range(1, HPD):
            need(HPD + h, (6, 2))
            cached_work(h, (6, 2))
        last(HPD)
        need(HPD, (5, 3))
        cached_work(0, (5, 3))
        last(HPD + 1)
        need(HPD + 1, (5, 3))
        cached_work(1, (5, 3))
        last(HPD + 2)
        need(HPD + 2, (5, 3))
        cached_work(2, (5, 3))
        for h in range(HPD):
            need(HPD + h, (4,))
            cached_work(h, (4,), rows=theirs)
            share(h)
        for h in range(HPD):
            cached_work(h, (4,), rows=mine)

    for h in range(HPD):
        o_copy(h).wait_recv()
        st_copy(h).wait_recv()
        m0 = mx[h, 0:TOK]
        l0 = sm[h, 0:TOK]
        m1 = jnp.broadcast_to(srecv[h, 0:1], (TOK, DH)).T
        l1 = jnp.broadcast_to(srecv[h, 1:2], (TOK, DH)).T
        m = jnp.maximum(m0, m1)
        w0 = jnp.exp2((m0 - m) * SCALE)
        w1 = jnp.exp2((m1 - m) * SCALE) * l1
        full = acc[h, 0:TOK] * w0 + orecv[h].astype(jnp.float32) * w1
        o_ref[:, h * DH : (h + 1) * DH] = (full / (l0 * w0 + w1)).astype(o_ref.dtype)

    def drain(h):
        for d in range(3):
            n_copy(8 - d if d else 0, 7 - d, h, None, right).wait_send()
            n_copy(d, d + 1, h, None, left).wait_send()
        n_copy(5, 4, h, 0, right).wait_send()
        n_copy(3, 4, h, 1, left).wait_send()
        for rel_y in range(NY):
            n_sib(rel_y, h).wait_send()

    for h in range(HPD):
        drain(h)
        q_copy(h).wait_send()
        o_copy(h).wait_send()
        st_copy(h).wait_send()

    @pl.when(first_half)
    def _():
        for r in range(1, heads_n):
            a2a_near(r).wait_send()
        for h in range(HPD, 2 * HPD):
            drain(h)

    @pl.when(second_half)
    def _():
        for r in range(heads_n):
            a2a_far(r).wait_send()


def per_device(heads_n, seq_n, *args):
    import functools

    hbm = pl.BlockSpec(memory_space=pltpu.HBM)
    vmem = pl.BlockSpec(memory_space=pltpu.VMEM)
    dma = pltpu.SemaphoreType.DMA
    f32, bf16 = jnp.float32, jnp.bfloat16
    return pl.pallas_call(
        functools.partial(kernel, heads_n, seq_n),
        out_shape=jax.ShapeDtypeStruct((TOK, HPD * DH), bf16),
        in_specs=[hbm] * 8,
        out_specs=vmem,
        scratch_shapes=[
            pltpu.VMEM((HPD, 2 * TOK, DH), bf16),
            pltpu.VMEM((NY, 2 * HPD, 2, 2 * TOK, DH), bf16),
            pltpu.VMEM((heads_n, 2, SBLK, HPD * DH), bf16),
            pltpu.VMEM((2, heads_n, 2, SBLK, HPD * DH), bf16),
            pltpu.VMEM((2, 2 * CTOK, HPD * DH), f32),
            pltpu.VMEM((2 * TOK, NY * 4 * CTOK), f32),
            pltpu.VMEM((HPD, 2 * TOK, DH), f32),
            pltpu.VMEM((HPD, 2 * TOK, DH), f32),
            pltpu.VMEM((HPD, 2 * TOK, DH), f32),
            pltpu.VMEM((HPD, TOK, DH), bf16),
            pltpu.VMEM((HPD, TOK, DH), bf16),
            pltpu.VMEM((HPD, 2, DH), f32),
            pltpu.VMEM((HPD, 2, DH), f32),
            pltpu.VMEM((SBLK, heads_n * HPD * DH), bf16),
            pltpu.VMEM((SBLK, heads_n * HPD * DH), bf16),
            pltpu.VMEM((1, heads_n * HPD), jnp.int32),
            pltpu.VMEM((1, heads_n * HPD), jnp.int32),
            pltpu.VMEM(args[7].shape, jnp.int32),
            dma((3, HPD)),
            dma((5,)),
            pltpu.SemaphoreType.REGULAR,
            pltpu.SemaphoreType.REGULAR,
            dma((heads_n,)),
            dma((2, heads_n)),
            dma((HPD,)),
            dma((HPD,)),
            dma((NY, 2 * HPD, 2)),
            dma((NY, 2 * HPD, 2)),
            dma((NY, 2 * HPD)),
            dma((NY, 2 * HPD)),
            dma((HPD,)),
            dma((HPD,)),
            dma((HPD,)),
            dma((HPD,)),
        ],
        compiler_params=pltpu.CompilerParams(
            collective_id=0, has_side_effects=True, vmem_limit_bytes=60 * 1024 * 1024
        ),
        name="attend_ring",
    )(*args)


def solution(mesh):
    import functools

    both = P(("seq", "head"), None)
    own = P("seq", "head")
    return jax.shard_map(
        functools.partial(per_device, mesh.shape["head"], mesh.shape["seq"]),
        mesh=mesh,
        in_specs=(own, own, own, both, both, both, both, P()),
        out_specs=own,
        check_vma=False,
    )
```

time: 54.9 us -> 53 us (0.965); the launches traced: 54.8 us -> 52.3 us
  Pallas kernels: 53.2 us -> 50.7 us
    pallas_call x1, Pallas kernels: 53.2 us -> 50.7 us  [per_device(): pl.pallas_call(functools.partial(kernel, heads_n, seq_n), out_shape=jax.S...]
where the time goes in v3:
time: 53 us; the launch traced here: 52.3 us
  Pallas kernels  50.7 us (96%)
  local copies, waits for them, and re-layouts  1.54 us (3%)
    pallas_call x1, Pallas kernels, per_device(): pl.pallas_call(functools.partial(kernel, heads_n, seq_n), out_shape=jax.S...  50.7 us
    unnamed x1, local copies, waits for them, and re-layouts  1.54 us

profile of v3, /device:TPU:1, one launch (start us, length us, event | category | flops | bytes accessed | tf_op | source)
XLA Modules:
  0.0 52.3 jit_solution(7031687729646094588)
XLA Ops:
  0.0 50.7 %attend_ring.1 = bf16[128,384]{1,0:T(8,128)(2,1)} custom-call(bf16[128,384]{1,0:T(8,128)(2,1)} %q_in.1, bf16[128,384]{1,0:T(8,128)(2,1)} %k_in.1, bf16[128,384]{1,0:T(8,128)(2,1)} %v_in.1, bf16[4,6144]{1,0:T(4,128)(2,1)} %ck_in.1, bf16[4,6144]{1,0:T(4,128)(2,1)} %cv_in.1, s32[1,48]{1,0:T(1,128)} %ke_in.1, s32[1,48]{1,0:T(1,128)} %ve_in.1, s32[64,64]{1,0:T(8,128)} %mask_in.1), custom_call_target="tpu_custom_call" | custom-call | tf_op jit(solution)/shard_map/attend_ring/pallas_call | solution.py:458
  50.7 1.5 %copy.10 = bf16[128,384]{1,0:T(8,128)(2,1)} copy(bf16[128,384]{1,0:T(8,128)(2,1)} %attend_ring.1) | data formatting | bytes 196608

commit v4 on v3

--- a/solution.py
+++ b/solution.py
@@ -323,6 +323,8 @@
         new_work(h, (0, 7, 1), rows=mine, first=True)
     for h in range(HPD):
         relay(3, h)
+        need(h, (6, 2))
+        new_work(h, (6, 2), rows=mine)
 
     @pl.when(first_half)
     def _():
@@ -359,53 +361,53 @@
     @pl.when(second_half)
     def _():
         for h in range(HPD):
-            need(h, (6, 2, 5, 3))
-            new_work(h, (6, 2, 5, 3))
-            need(h, (4,))
-            new_work(h, (4,))
+            need(h, (5, 3, 4))
+            new_work(h, (6, 2, 5, 3, 4), rows=theirs)
             share(h)
+        for h in range(HPD):
+            new_work(h, (5, 3, 4), rows=mine)
 
     @pl.when(first_half)
     def _():
         for h in range(HPD):
             relay(1, HPD + h)
-            need(h, (6, 2, 5, 3))
-            new_work(h, (6, 2, 5, 3))
+            need(h, (5, 3, 4))
+            new_work(h, (6, 2, 5, 3, 4), rows=theirs)
         relay(2, HPD)
         for h in range(HPD):
-            need(h, (4,))
-            new_work(h, (4,))
+            new_work(h, (5, 3, 4), rows=mine)
         relay(2, HPD + 1)
         need(HPD, (0, 7, 1))
         cached_work(0, (0, 7, 1))
         relay(2, HPD + 2)
         need(HPD + 1, (0, 7, 1))
         cached_work(1, (0, 7, 1))
+        need(HPD, (6, 2))
+        cached_work(0, (6, 2))
         relay(3, HPD)
         need(HPD + 2, (0, 7, 1))
         cached_work(2, (0, 7, 1))
         relay(3, HPD + 1)
-        need(HPD, (6, 2))
-        cached_work(0, (6, 2))
-        relay(3, HPD + 2)
         for h in range(1, HPD):
             need(HPD + h, (6, 2))
             cached_work(h, (6, 2))
-        last(HPD)
+        relay(3, HPD + 2)
         need(HPD, (5, 3))
         cached_work(0, (5, 3))
-        last(HPD + 1)
+        last(HPD)
         need(HPD + 1, (5, 3))
         cached_work(1, (5, 3))
+        last(HPD + 1)
+        need(HPD, (4,))
+        cached_work(0, (4,))
+        share(0)
         last(HPD + 2)
         need(HPD + 2, (5, 3))
         cached_work(2, (5, 3))
-        for h in range(HPD):
+        for h in range(1, HPD):
             need(HPD + h, (4,))
-            cached_work(h, (4,), rows=theirs)
+            cached_work(h, (4,))
             share(h)
-        for h in range(HPD):
-            cached_work(h, (4,), rows=mine)
 
     for h in range(HPD):
         o_copy(h).wait_recv()

time: 53 us -> 52.6 us (level); the launches traced: 52.3 us -> 52.4 us
  no operation moved by 1% of the time
where the time goes in v4:
time: 52.6 us; the launch traced here: 52.4 us
  Pallas kernels  50.9 us (97%)
  local copies, waits for them, and re-layouts  1.54 us (3%)
    pallas_call x1, Pallas kernels, per_device(): pl.pallas_call(functools.partial(kernel, heads_n, seq_n), out_shape=jax.S...  50.9 us
    unnamed x1, local copies, waits for them, and re-layouts  1.54 us

profile of v4, /device:TPU:1, one launch (start us, length us, event | category | flops | bytes accessed | tf_op | source)
XLA Modules:
  0.0 52.4 jit_solution(4799961390945810683)
XLA Ops:
  0.0 50.9 %attend_ring.1 = bf16[128,384]{1,0:T(8,128)(2,1)} custom-call(bf16[128,384]{1,0:T(8,128)(2,1)} %q_in.1, bf16[128,384]{1,0:T(8,128)(2,1)} %k_in.1, bf16[128,384]{1,0:T(8,128)(2,1)} %v_in.1, bf16[4,6144]{1,0:T(4,128)(2,1)} %ck_in.1, bf16[4,6144]{1,0:T(4,128)(2,1)} %cv_in.1, s32[1,48]{1,0:T(1,128)} %ke_in.1, s32[1,48]{1,0:T(1,128)} %ve_in.1, s32[64,64]{1,0:T(8,128)} %mask_in.1), custom_call_target="tpu_custom_call" | custom-call | tf_op jit(solution)/shard_map/attend_ring/pallas_call | solution.py:460
  50.9 1.5 %copy.10 = bf16[128,384]{1,0:T(8,128)(2,1)} copy(bf16[128,384]{1,0:T(8,128)(2,1)} %attend_ring.1) | data formatting | bytes 196608
